TPU v7x, 32 devices: a whole 2x2x4 slice. The times are simulated.
32 devices in a mesh: fsdp: 8 (over z, x), ctx: 4 (over y, core).
Axes of the slice: x: 2, y: 2, z: 4, core: 2. Of those that a mesh axis runs over, the one named last changes fastest.
Arguments:
- inputs: bfloat16 [4096, 768], P(('fsdp', 'ctx')), may hold values from -6 to 6
- lengths: int32 [8, 3], P('fsdp'), may hold values from 1 to 384, 512 in all within a row
- norm1_gain: bfloat16 [768], P(('fsdp', 'ctx')), may hold values from 0.5 to 1.5
- qkv_weight: bfloat16 [768, 2304], P(('fsdp', 'ctx'))
- attn_out_weight: bfloat16 [768, 768], P(('fsdp', 'ctx')), may hold values from -2.5 to 2.5
- norm2_gain: bfloat16 [768], P(('fsdp', 'ctx')), may hold values from 0.5 to 1.5
- ffn_in_weight: bfloat16 [768, 2304], P(('fsdp', 'ctx')), may hold values from -0.21875 to 0.21875
- ffn_out_weight: bfloat16 [1152, 768], P(None, ('fsdp', 'ctx')), may hold values from -0.1875 to 0.1875
- out_grad: bfloat16 [4096, 768], P(('fsdp', 'ctx')), may hold values from -6 to 6
Outputs:
- outputs: bfloat16 [4096, 768], P(('fsdp', 'ctx'))
- input_grad: bfloat16 [4096, 768], P(('fsdp', 'ctx'))
- norm1_gain_grad: float32 [768], P(('fsdp', 'ctx'))
- qkv_weight_grad: float32 [768, 2304], P(('fsdp', 'ctx'))
- attn_out_weight_grad: float32 [768, 768], P(('fsdp', 'ctx'))
- norm2_gain_grad: float32 [768], P(('fsdp', 'ctx'))
- ffn_in_weight_grad: float32 [768, 2304], P(('fsdp', 'ctx'))
- ffn_out_weight_grad: float32 [1152, 768], P(None, ('fsdp', 'ctx'))
Inputs may be any that keep to these rules, and one draw needn't show every extreme that they name: `lengths`: each row sums to 512, and its largest entry is exactly 384.
All inputs are finite; a program needn't handle non-finite values.
Results may differ from a plain program's by a relative error of at most 0.038.
The roundings to bfloat16 on the way count: a program that leaves them out, or rounds other values in their place, can miss the bound.
Values may be sent and summed in bfloat16 or wider, within the bound.
No kernel may reach another device: no remote copies, remote signals or barrier semaphores. Data moves between devices by JAX's collectives and lax.ppermute only.
A program may use at most 128 MiB of HBM per device.

v0:
```python
import math
import jax
import jax.numpy as jnp
from jax import lax
from jax.sharding import PartitionSpec as P

rope_base = 160000.0
norm_eps = 1e-05
score_scale = 0.125


def positions(length_row, index_rows):
    seq_ends = jnp.cumsum(length_row)
    starts = seq_ends - length_row
    segment = jnp.sum((index_rows[:, None] >= seq_ends[None, :]).astype(jnp.int32), axis=1)
    seq_numbers = jnp.arange(length_row.shape[0], dtype=jnp.int32)
    seq_start = jnp.sum(
        jnp.where(segment[:, None] == seq_numbers[None, :], starts[None, :], 0), axis=1
    )
    return (segment, index_rows - seq_start)


def rope_tables(places):
    freq_steps = jnp.arange(32, dtype=jnp.float32)
    frequency = jnp.exp(freq_steps * (-2.0 / 64.0) * math.log(rope_base))
    angles = places.astype(jnp.float32)[:, None] * frequency[None, :]
    angles = jnp.concatenate([angles, angles], axis=1)
    return (jnp.cos(angles), jnp.sin(angles))


def rotate(values_in, cosine, sine_tab):
    half_width = values_in.shape[-1] // 2
    turned = jnp.concatenate([-values_in[..., half_width:], values_in[..., :half_width]], axis=-1)
    return values_in * cosine[:, None, :] + turned * sine_tab[:, None, :]


def unrotate(values_in, cosine, sine_tab):
    half_width = values_in.shape[-1] // 2
    scaled = values_in * sine_tab[:, None, :]
    turned_back = jnp.concatenate([scaled[..., half_width:], -scaled[..., :half_width]], axis=-1)
    return values_in * cosine[:, None, :] + turned_back


def layer_norm(values_in):
    average = jnp.mean(values_in, axis=-1, keepdims=True)
    centred = values_in - average
    spread = jnp.mean(centred * centred, axis=-1, keepdims=True)
    inv_scale = lax.rsqrt(spread + norm_eps)
    return (centred * inv_scale, inv_scale)


def norm_back(grad_h, normed, inv_scale, gain_row):
    grad_n = grad_h * gain_row
    return inv_scale * (
        grad_n
        - jnp.mean(grad_n, axis=-1, keepdims=True)
        - normed * jnp.mean(grad_n * normed, axis=-1, keepdims=True)
    )


def gelu_parts(gate_in):
    normal_cdf = 0.5 * (1.0 + lax.erf(gate_in * (1.0 / math.sqrt(2.0))))
    normal_pdf = jnp.exp(-0.5 * gate_in * gate_in) * (1.0 / math.sqrt(2.0 * math.pi))
    return (gate_in * normal_cdf, normal_cdf + gate_in * normal_pdf)


def contract_rows(left_side, right_side):
    return lax.dot_general(
        left_side, right_side, (((0,), (0,)), ((), ())), preferred_element_type=jnp.float32
    )


def contract_last(left_side, right_side):
    return lax.dot_general(
        left_side, right_side, (((1,), (1,)), ((), ())), preferred_element_type=jnp.float32
    )


def block_scores(block_query, head_keys, segment):
    scores = contract_last(block_query, head_keys) * score_scale
    allowed = segment[:, None] == segment[None, :]
    return jnp.where(allowed, scores, -1e30)


def attend(queries, key_rows, value_rows, segment, block_rows):
    head_outs = []
    head_sums = []
    for head_index in range(queries.shape[1] // 64):
        head_cols = slice(64 * head_index, 64 * head_index + 64)
        head_keys = key_rows[:, head_cols]
        head_values = value_rows[:, head_cols]
        block_query = queries[0:block_rows, head_cols]
        scores = block_scores(block_query, head_keys, segment)
        row_top = jnp.max(scores, axis=1, keepdims=True)
        logsum = row_top + jnp.log(jnp.sum(jnp.exp(scores - row_top), axis=1, keepdims=True))
        prob_block = jnp.exp(scores - logsum).astype(jnp.bfloat16)
        rows_out = jnp.dot(prob_block, head_values, preferred_element_type=jnp.float32).astype(
            jnp.bfloat16
        )
        rows_sum = logsum[:, 0]
        head_outs.append(rows_out)
        head_sums.append(rows_sum)
    return (jnp.concatenate(head_outs, axis=1), jnp.stack(head_sums))


def attend_back(queries, key_rows, value_rows, attended, grad_att, logsums, segment, block_rows):
    grads_q = []
    grads_k = []
    grads_v = []
    for head_index in range(queries.shape[1] // 64):
        head_cols = slice(64 * head_index, 64 * head_index + 64)
        head_query = queries[:, head_cols]
        head_keys = key_rows[:, head_cols]
        head_values = value_rows[:, head_cols]
        head_grad = grad_att[:, head_cols]
        row_delta = jnp.sum(
            head_grad.astype(jnp.float32) * attended[:, head_cols].astype(jnp.float32), axis=1
        )
        scores = block_scores(head_query, head_keys, segment)
        prob_full = jnp.exp(scores - logsums[head_index, 0:block_rows][:, None])
        grad_v = contract_rows(prob_full.astype(jnp.bfloat16), head_grad)
        grad_p = contract_last(head_grad, head_values)
        grad_s = (prob_full * (grad_p - row_delta[0:block_rows, None])).astype(jnp.bfloat16)
        query_blocks = jnp.dot(grad_s, head_keys, preferred_element_type=jnp.float32) * score_scale
        grad_k = contract_rows(grad_s, head_query) * score_scale
        grads_q.append(query_blocks)
        grads_k.append(grad_k)
        grads_v.append(grad_v)
    return (
        jnp.concatenate(grads_q, axis=1),
        jnp.concatenate(grads_k, axis=1),
        jnp.concatenate(grads_v, axis=1),
    )


def local(
    inputs,
    lengths,
    norm1_gain,
    qkv_weight,
    attn_out_weight,
    norm2_gain,
    ffn_in_weight,
    ffn_out_weight,
    out_grad,
):
    f32 = jnp.float32
    bf16 = jnp.bfloat16
    tok_dev = inputs.shape[0]
    model_width = inputs.shape[1]
    head_count = model_width // 64
    ctx_count = lax.axis_size("ctx")
    local_width = model_width // ctx_count
    local_heads = local_width // 64
    group_rows = tok_dev * ctx_count
    block_rows = 512
    shards = (norm1_gain, qkv_weight, attn_out_weight, norm2_gain, ffn_in_weight, ffn_out_weight)
    gain_one, w_qkv, w_attn, gain_two, w_in, w_out = (
        lax.all_gather(shards[0], ("fsdp", "ctx"), axis=0, tiled=True),
        lax.all_gather(shards[1], ("fsdp", "ctx"), axis=0, tiled=True),
        lax.all_gather(shards[2], ("fsdp", "ctx"), axis=0, tiled=True),
        lax.all_gather(shards[3], ("fsdp", "ctx"), axis=0, tiled=True),
        lax.all_gather(shards[4], ("fsdp", "ctx"), axis=0, tiled=True),
        lax.all_gather(shards[5], ("fsdp", "ctx"), axis=1, tiled=True),
    )
    index_rows = jnp.arange(group_rows, dtype=jnp.int32)
    segment, group_places = positions(lengths[0], index_rows)
    cos_group, sin_group = rope_tables(group_places)
    resid_in = inputs.astype(f32)
    normed_one, scale_one = layer_norm(resid_in)
    hidden_one = (normed_one * gain_one.astype(f32)).astype(bf16)
    local_places = lax.dynamic_slice_in_dim(group_places, lax.axis_index("ctx") * tok_dev, tok_dev)
    cos_local, sin_local = rope_tables(local_places)
    joined_out = jnp.dot(hidden_one, w_qkv, preferred_element_type=f32)
    queries = rotate(
        joined_out[:, :model_width].reshape(tok_dev, head_count, 64), cos_local, sin_local
    )
    queries = queries.reshape(tok_dev, model_width).astype(bf16)
    key_rows = rotate(
        joined_out[:, model_width : 2 * model_width].reshape(tok_dev, head_count, 64),
        cos_local,
        sin_local,
    )
    key_rows = key_rows.reshape(tok_dev, model_width).astype(bf16)
    value_rows = joined_out[:, 2 * model_width :].astype(bf16)
    query_heads, key_heads, value_heads = (
        lax.all_to_all(queries, "ctx", split_axis=1, concat_axis=0, tiled=True),
        lax.all_to_all(key_rows, "ctx", split_axis=1, concat_axis=0, tiled=True),
        lax.all_to_all(value_rows, "ctx", split_axis=1, concat_axis=0, tiled=True),
    )
    attended_heads, logsums = attend(query_heads, key_heads, value_heads, segment, block_rows)
    attended = lax.all_to_all(attended_heads, "ctx", split_axis=0, concat_axis=1, tiled=True)
    resid_mid = resid_in + jnp.dot(attended, w_attn, preferred_element_type=f32)
    normed_two, scale_two = layer_norm(resid_mid)
    hidden_two = (normed_two * gain_two.astype(f32)).astype(bf16)
    expanded = jnp.dot(hidden_two, w_in, preferred_element_type=f32)
    hidden_units = w_out.shape[0]
    gate_in = expanded[:, :hidden_units]
    up_in = expanded[:, hidden_units:]
    activated, gelu_slope = gelu_parts(gate_in)
    mixed_act = (activated * up_in).astype(bf16)
    outputs = (resid_mid + jnp.dot(mixed_act, w_out, preferred_element_type=f32)).astype(bf16)
    grad_mixed = contract_last(out_grad, w_out)
    grad_expanded = jnp.concatenate(
        [grad_mixed * up_in * gelu_slope, grad_mixed * activated], axis=1
    ).astype(bf16)
    grad_hidden_two = contract_last(grad_expanded, w_in)
    grad_gain_two = jnp.sum(grad_hidden_two * normed_two, axis=0)
    grad_mid = out_grad.astype(f32) + norm_back(
        grad_hidden_two, normed_two, scale_two, gain_two.astype(f32)
    )
    grad_mid_half = grad_mid.astype(bf16)
    grad_att = contract_last(grad_mid_half, w_attn).astype(bf16)
    grad_att_heads = lax.all_to_all(grad_att, "ctx", split_axis=1, concat_axis=0, tiled=True)
    grad_q_heads, grad_k_heads, grad_v_heads = attend_back(
        query_heads,
        key_heads,
        value_heads,
        attended_heads,
        grad_att_heads,
        logsums,
        segment,
        block_rows,
    )
    grad_q_heads = unrotate(grad_q_heads.reshape(group_rows, local_heads, 64), cos_group, sin_group)
    grad_q_heads = grad_q_heads.reshape(group_rows, local_width).astype(bf16)
    grad_k_heads = unrotate(grad_k_heads.reshape(group_rows, local_heads, 64), cos_group, sin_group)
    grad_k_heads = grad_k_heads.reshape(group_rows, local_width).astype(bf16)
    grad_v_heads = grad_v_heads.astype(bf16)
    grad_q, grad_k, grad_v = (
        lax.all_to_all(grad_q_heads, "ctx", split_axis=0, concat_axis=1, tiled=True),
        lax.all_to_all(grad_k_heads, "ctx", split_axis=0, concat_axis=1, tiled=True),
        lax.all_to_all(grad_v_heads, "ctx", split_axis=0, concat_axis=1, tiled=True),
    )
    grad_joined = jnp.concatenate([grad_q, grad_k, grad_v], axis=1)
    grad_hidden_one = contract_last(grad_joined, w_qkv)
    every_sum = lax.psum_scatter(
        jnp.concatenate(
            [
                contract_rows(hidden_one, grad_joined),
                jnp.concatenate(
                    [
                        contract_rows(attended, grad_mid_half),
                        contract_rows(hidden_two, grad_expanded),
                        contract_rows(out_grad, mixed_act),
                    ],
                    axis=1,
                ),
            ],
            axis=1,
        ),
        ("fsdp", "ctx"),
        scatter_dimension=0,
        tiled=True,
    )
    sum_w_qkv = every_sum[:, : 3 * model_width]
    rest_sums = every_sum[:, 3 * model_width :]
    grad_gain_one = jnp.sum(grad_hidden_one * normed_one, axis=0)
    input_grad = (
        grad_mid + norm_back(grad_hidden_one, normed_one, scale_one, gain_one.astype(f32))
    ).astype(bf16)
    sum_gain_one, sum_gain_two = (
        lax.psum_scatter(grad_gain_one, ("fsdp", "ctx"), scatter_dimension=0, tiled=True),
        lax.psum_scatter(grad_gain_two, ("fsdp", "ctx"), scatter_dimension=0, tiled=True),
    )
    sum_w_attn = rest_sums[:, :model_width]
    sum_w_in = rest_sums[:, model_width : model_width + 2 * hidden_units]
    sum_w_out = rest_sums[:, model_width + 2 * hidden_units :].T
    return (
        outputs,
        input_grad,
        sum_gain_one,
        sum_w_qkv,
        sum_w_attn,
        sum_gain_two,
        sum_w_in,
        sum_w_out,
    )


def solution(mesh):
    in_specs = (
        P(("fsdp", "ctx"), None),
        P("fsdp", None),
        P(("fsdp", "ctx")),
        P(("fsdp", "ctx"), None),
        P(("fsdp", "ctx"), None),
        P(("fsdp", "ctx")),
        P(("fsdp", "ctx"), None),
        P(None, ("fsdp", "ctx")),
        P(("fsdp", "ctx"), None),
    )
    out_specs = (
        P(("fsdp", "ctx"), None),
        P(("fsdp", "ctx"), None),
        P(("fsdp", "ctx")),
        P(("fsdp", "ctx"), None),
        P(("fsdp", "ctx"), None),
        P(("fsdp", "ctx")),
        P(("fsdp", "ctx"), None),
        P(None, ("fsdp", "ctx")),
    )
    return jax.shard_map(local, mesh=mesh, in_specs=in_specs, out_specs=out_specs, check_vma=False)
```

profile of v0, /device:TPU:0, one launch (start us, length us, event | category | flops | bytes accessed | tf_op | source)
XLA Modules:
  0.0 649.4 jit_solution(332151156606937224)
XLA Ops:
  11.9 42.2 %all-reduce.6 = (bf16[768]{0:T(1024)(128)(2,1)S(1)}, bf16[768]{0:T(1024)(128)(2,1)}) all-reduce(bf16[768]{0:T(1024)(128)(2,1)S(1)} %dynamic-update-slice, bf16[768]{0:T(1024)(128)(2,1)S(1)} %dynamic-update-slice.1), channel_id=1, replica_groups=mesh['fsdp'=8,'ctx'=4] {'fsdp','ctx'}, use_global_device_ids=true, to_apply=%add | all-reduce | flops 1536 | bytes 6144
  56.3 17.7 %all-gather.5.cloned.1.call-done = bf16[768,2304]{1,0:T(8,128)(2,1)} async-done(((bf16[24,2304]{1,0:T(8,128)(2,1)}), bf16[768,2304]{1,0:T(8,128)(2,1)}) %all-gather.5.cloned.1.call-update) | async-done | bytes 3538960 | tf_op jit(solution)/shard_map/all_gather | solution.py:160
  73.9 2.7 fusion.85
  78.5 3.4 all-to-all-start
  84.1 3.2 all-to-all-done
  87.3 3.4 all-to-all-start.1
  90.7 5.2 all-to-all-done.1
  96.0 3.4 all-to-all-start.2
  101.2 3.7 all-to-all-done.2
  107.5 3.4 all-to-all-start.3
  112.7 1.9 mul.371
  114.6 14.8 %all-gather.7.cloned.1.call-done = bf16[768,768]{1,0:T(8,128)(2,1)} async-done(((bf16[24,768]{1,0:T(8,128)(2,1)}), bf16[768,768]{1,0:T(8,128)(2,1)}) %all-gather.7.cloned.1.call-update) | async-done | bytes 1179664 | tf_op jit(solution)/shard_map/all_gather | solution.py:161
  130.1 1.8 fusion.95
  133.1 58.2 %all-gather.9.cloned.1.call-done = bf16[768,2304]{1,0:T(8,128)(2,1)} async-done(((bf16[24,2304]{1,0:T(8,128)(2,1)}), bf16[768,2304]{1,0:T(8,128)(2,1)}) %all-gather.9.cloned.1.call-update) | async-done | bytes 3538960 | tf_op jit(solution)/shard_map/all_gather | solution.py:163
  191.3 3.8 fusion.87
  195.0 53.2 %all-gather.11.cloned.1.call-done = bf16[1152,768]{0,1:T(8,128)(2,1)} async-done(((bf16[1152,24]{0,1:T(8,128)(2,1)}), bf16[1152,768]{0,1:T(8,128)(2,1)}) %all-gather.11.cloned.1.call-update) | async-done | bytes 1769488 | tf_op jit(solution)/shard_map/all_gather | solution.py:164
  248.3 2.6 fusion.18
  251.2 1.9 multiply_reduce_fusion
  254.5 2.2 convolution_convert_fusion
  256.8 1.7 copy.116
  258.5 4.2 all-to-all-start.4
  262.7 5.1 fusion.37
  267.9 0.9 copy_bitcast_fusion
  268.8 1.0 multiply_reduce_fusion.7
  269.8 0.9 fusion.8
  270.8 0.9 fusion.7
  271.7 0.9 fusion.9
  280.3 3.4 all-to-all-start.7
  284.8 1.6 fusion.34
  287.1 1.8 all-to-all-done.7
  288.9 3.4 all-to-all-start.5
  292.3 2.5 convolution_bitcast_fusion
  295.6 2.0 all-to-all-done.5
  297.6 4.0 all-to-all-start.6
  301.6 3.2 fusion.49
  304.8 2.1 all-to-all-done.6
  307.0 2.5 fusion.39
  309.5 1.0 copy-done
  311.2 7.4 %pad_maximum_fusion = f32[768,6528]{1,0:T(8,128)} fusion(f32[768,1152]{1,0:T(8,128)S(1)} %copy-done, f32[768,2304]{1,0:T(8,128)S(1)} %bitcast.116, f32[768,768]{1,0:T(8,128)S(1)} %copy-done.1, f32[768,2304]{1,0:T(8,128)S(1)} %fusion.39), kind=kLoop, calls=%fused_computation | loop fusion | flops 15040512 | bytes 40108032 | tf_op jit(solution)/shard_map/concatenate | solution.py:238
  318.7 1.2 copy-done.6
  319.9 2.8 fusion.6
  322.7 4.3 fusion.31
  327.1 39.3 %all-reduce.5 = (f32[768]{0:T(1024)S(1)}, f32[768]{0:T(1024)S(1)}) all-reduce(f32[768]{0:T(1024)S(1)} %get-tuple-element.10, f32[768]{0:T(1024)S(1)} %copy-done.41), channel_id=2, replica_groups=mesh['fsdp'=8,'ctx'=4] {'fsdp','ctx'}, use_global_device_ids=true, to_apply=%region_21.22.clone | all-reduce | flops 1536 | bytes 12288
  367.5 1.9 fusion.30
  369.4 268.4 %all-reduce.9.cloned.1.call-done = f32[768,6528]{1,0:T(8,128)} async-done(((f32[768,6528]{1,0:T(8,128)}), f32[768,6528]{1,0:T(8,128)}) %all-reduce.9.cloned.1.call-update) | async-done | bytes 20054032
  637.8 1.6 dynamic-slice.4
  639.4 1.6 dynamic-slice_bitcast_fusion
  641.0 1.9 fusion.88
  (197 shorter events, 32.6 us)
Async XLA Ops:
  7.2 48.8 %copy-start.2 = (bf16[128,768]{1,0:T(8,128)(2,1)S(1)}, bf16[128,768]{1,0:T(8,128)(2,1)}, u32[]{:S(2)}) copy-start(bf16[128,768]{1,0:T(8,128)(2,1)} %param.9) | copy-start | bytes 589828
  7.2 66.8 %all-gather.5.cloned.1.call-start = ((), (), s32[]{:S(2)}) async-start(), calls=%async_computation.8 | async-start | bytes 3649536 | tf_op jit(solution)/shard_map/all_gather | solution.py:160
  7.9 121.5 %all-gather.7.cloned.1.call-start = ((), (), s32[]{:S(2)}) async-start(), calls=%async_computation.9 | async-start | bytes 1216512 | tf_op jit(solution)/shard_map/all_gather | solution.py:161
  8.7 182.6 %all-gather.9.cloned.1.call-start = ((), (), s32[]{:S(2)}) async-start(), calls=%async_computation.10 | async-start | bytes 3649536 | tf_op jit(solution)/shard_map/all_gather | solution.py:163
  54.1 22.5 %copy-start.42 = (f32[32]{0:T(128)}, f32[32]{0:T(128)S(1)}, u32[]{:S(2)}) copy-start(f32[32]{0:T(128)S(1)} %multiply_exponential_fusion) | copy-start | bytes 388
  56.1 20.6 %copy-start.33 = (f32[128]{0:T(128)}, f32[128]{0:T(128)S(1)}, u32[]{:S(2)}) copy-start(f32[128]{0:T(128)S(1)} %broadcast_multiply_fusion.9) | copy-start | bytes 1540
  56.3 20.4 %copy-start.37 = (f32[128]{0:T(128)}, f32[128]{0:T(128)S(1)}, u32[]{:S(2)}) copy-start(f32[128]{0:T(128)S(1)} %add_rsqrt_fusion.1) | copy-start | bytes 1540
  78.5 8.8 %all-to-all-start = ((bf16[128,4,192]{0,2,1:T(8,128)(2,1)}), bf16[128,4,192]{0,2,1:T(8,128)(2,1)S(1)}, u32[]{:S(2)}, u32[]{:S(2)}) async-start(bf16[128,4,192]{0,2,1:T(8,128)(2,1)} %bitcast.7), calls=%async_computation | async-start | bytes 393216 | tf_op jit(solution)/shard_map/all_to_all | solution.py:187
  81.9 166.4 %all-gather.11.cloned.1.call-start = ((), (), s32[]{:S(2)}) async-start(), calls=%async_computation.11 | async-start | bytes 1824768 | tf_op jit(solution)/shard_map/all_gather | solution.py:164
  87.3 8.6 %all-to-all-start.1 = ((bf16[128,4,192]{0,2,1:T(8,128)(2,1)}), bf16[128,4,192]{0,2,1:T(8,128)(2,1)S(1)}, u32[]{:S(2)}, u32[]{:S(2)}) async-start(bf16[128,4,192]{0,2,1:T(8,128)(2,1)} %bitcast.11), calls=%async_computation.1 | async-start | bytes 393216 | tf_op jit(solution)/shard_map/all_to_all | solution.py:188
  90.7 9.4 %copy-start.14 = (bf16[512,192]{0,1:T(8,128)(2,1)}, bf16[512,192]{0,1:T(8,128)(2,1)S(1)}, u32[]{:S(2)}) copy-start(bf16[512,192]{0,1:T(8,128)(2,1)S(1)} %copy_bitcast_fusion.2) | copy-start | bytes 589828
  96.0 8.9 %all-to-all-start.2 = ((bf16[128,4,192]{0,2,1:T(8,128)(2,1)}), bf16[128,4,192]{0,2,1:T(8,128)(2,1)S(1)}, u32[]{:S(2)}, u32[]{:S(2)}) async-start(bf16[128,4,192]{0,2,1:T(8,128)(2,1)} %bitcast.13), calls=%async_computation.2 | async-start | bytes 393216 | tf_op jit(solution)/shard_map/all_to_all | solution.py:189
  101.1 4.7 copy-start.31
  105.2 5.7 copy-start.40
  105.2 5.7 copy-start.43
  105.2 5.8 copy-start.44
  107.5 21.9 %all-to-all-start.3 = ((bf16[4,128,192]{1,2,0:T(8,128)(2,1)}), bf16[4,128,192]{1,2,0:T(8,128)(2,1)S(1)}, u32[]{:S(2)}, u32[]{:S(2)}) async-start(bf16[4,128,192]{1,2,0:T(8,128)(2,1)} %copy_bitcast_fusion.4), calls=%async_computation.3 | async-start | bytes 393216 | tf_op jit(solution)/shard_map/all_to_all | solution.py:192
  248.3 2.9 copy-start.7
  248.3 2.9 copy-start.36
  248.3 2.9 copy-start.39
  250.9 2.3 copy-start.26
  250.9 2.3 copy-start.27
  258.5 9.4 %all-to-all-start.4 = ((bf16[128,4,192]{0,2,1:T(8,128)(2,1)}), bf16[128,4,192]{0,2,1:T(8,128)(2,1)}, u32[]{:S(2)}, u32[]{:S(2)}) async-start(bf16[128,4,192]{0,2,1:T(8,128)(2,1)} %bitcast.126), calls=%async_computation.4 | async-start | bytes 393216 | tf_op jit(solution)/shard_map/all_to_all | solution.py:214
  267.8 3.9 copy-start.32
  269.8 2.8 copy-start.10
  270.8 2.2 copy-start.15
  274.9 4.6 copy-start.30
  275.2 4.3 copy-start.29
  275.2 4.3 copy-start.28
  276.6 7.0 %copy-start.25 = (f32[512,64]{0,1:T(8,128)S(1)}, f32[512,64]{0,1:T(8,128)}, u32[]{:S(2)}) copy-start(f32[512,64]{0,1:T(8,128)} %get-tuple-element.42) | copy-start | bytes 393220
  280.3 8.6 %all-to-all-start.7 = ((bf16[4,128,192]{1,2,0:T(8,128)(2,1)}), bf16[4,128,192]{1,2,0:T(8,128)(2,1)S(1)}, u32[]{:S(2)}, u32[]{:S(2)}) async-start(bf16[4,128,192]{1,2,0:T(8,128)(2,1)} %pad_maximum_fusion.11), calls=%async_computation.7 | async-start | bytes 393216 | tf_op jit(solution)/shard_map/all_to_all | solution.py:233
  284.8 7.5 %copy-start.5 = (f32[128,2304]{1,0:T(8,128)S(1)}, f32[128,2304]{1,0:T(8,128)}, u32[]{:S(2)}) copy-start(f32[128,2304]{1,0:T(8,128)} %fusion.87) | copy-start | bytes 3538948
  284.8 7.5 %copy-start.13 = (bf16[128,768]{1,0:T(8,128)(2,1)S(1)}, bf16[128,768]{1,0:T(8,128)(2,1)}, u32[]{:S(2)}) copy-start(bf16[128,768]{1,0:T(8,128)(2,1)} %param.17) | copy-start | bytes 589828
  288.9 5.9 copy-start.18
  288.9 8.6 %all-to-all-start.5 = ((bf16[4,128,192]{1,2,0:T(8,128)(2,1)}), bf16[4,128,192]{1,2,0:T(8,128)(2,1)S(1)}, u32[]{:S(2)}, u32[]{:S(2)}) async-start(bf16[4,128,192]{1,2,0:T(8,128)(2,1)} %copy.121), calls=%async_computation.5 | async-start | bytes 393216 | tf_op jit(solution)/shard_map/all_to_all | solution.py:231
  295.5 11.4 %copy-start.3 = (bf16[128,768]{1,0:T(8,128)(2,1)S(1)}, bf16[128,768]{1,0:T(8,128)(2,1)}, u32[]{:S(2)}) copy-start(bf16[128,768]{1,0:T(8,128)(2,1)} %param.9) | copy-start | bytes 589828
  295.6 11.4 %copy-start.34 = (f32[128]{0:T(128)S(1)}, f32[128]{0:T(128)}, u32[]{:S(2)}) copy-start(f32[128]{0:T(128)} %copy-done.33) | copy-start | bytes 1540
  295.6 11.4 %copy-start.38 = (f32[128]{0:T(128)S(1)}, f32[128]{0:T(128)}, u32[]{:S(2)}) copy-start(f32[128]{0:T(128)} %copy-done.37) | copy-start | bytes 1540
  297.6 4.0 copy-start.20
  297.6 9.4 %all-to-all-start.6 = ((bf16[4,128,192]{1,2,0:T(8,128)(2,1)}), bf16[4,128,192]{1,2,0:T(8,128)(2,1)}, u32[]{:S(2)}, u32[]{:S(2)}) async-start(bf16[4,128,192]{1,2,0:T(8,128)(2,1)} %copy.122), calls=%async_computation.6 | async-start | bytes 393216 | tf_op jit(solution)/shard_map/all_to_all | solution.py:232
  301.6 336.2 %all-reduce.9.cloned.1.call-start = ((), (), s32[]{:S(2)}) async-start(), calls=%async_computation.12 | async-start | bytes 40108032
  301.6 7.8 %slice-start = ((s8[7077888]{0:T(1024)(128)(4,1)}), s8[2883584]{0:T(1024)(128)(4,1)S(1)}, s32[]{:S(2)}) async-start(s8[7077888]{0:T(1024)(128)(4,1)} %bitcast.115), calls=%async_computation.13 | async-start | bytes 5767168
  306.9 2.5 slice-start.1
  307.0 3.6 copy-start
  307.0 4.2 copy-start.1
  318.6 4.1 copy-start.19
  318.7 4.1 copy-start.21
  322.7 4.3 copy-start.41
  (12 other events, 12.4 us)
Sparse Core Ops, SparseCore 0:
  10.9 63.0 all-gather.4
  76.8 52.5 all-gather.6
  132.3 58.9 all-gather.8
  194.0 54.2 all-gather.10
  318.8 318.9 all-reduce.8
where the time goes:
time: 651 us; the launch traced here: 649 us
  waiting for transfers between devices  433 us (67%)
  blocking collectives  81.5 us (13%)
  matrix products  42.7 us (7%)
  local copies, waits for them, and re-layouts  29.3 us (5%)
  starting transfers between devices  28.6 us (4%)
  other arithmetic  19.8 us (3%)
  between operations  14.6 us (2%)
    unnamed x6, waiting for transfers between devices  271 us
    unnamed x2, blocking collectives  81.5 us
    all_gather x1, waiting for transfers between devices, local(): lax.all_gather(shards[4], ('fsdp', 'ctx'), axis=0, tiled=True)  58.2 us
    all_gather x1, waiting for transfers between devices, local(): lax.all_gather(shards[5], ('fsdp', 'ctx'), axis=1, tiled=True)  53.2 us
    all_gather x1, waiting for transfers between devices, local(): lax.all_gather(shards[1], ('fsdp', 'ctx'), axis=0, tiled=True)  17.7 us
    dot_general x10, matrix products, contract_rows(): lax.dot_general(left_side, right_side, (((0,), (0,)), ((), ())), preferre...  17 us
    all_gather x1, waiting for transfers between devices, local(): lax.all_gather(shards[2], ('fsdp', 'ctx'), axis=0, tiled=True)  14.8 us
    dot_general x10, matrix products, contract_last(): lax.dot_general(left_side, right_side, (((1,), (1,)), ((), ())), preferre...  13.2 us
  transfers between devices with their start and end apart: 13, of which 11 were waited for; matrix products, arithmetic and copies ran while one was open for 7% of the time, Pallas kernels for 0%

commit v1 on v0

--- a/solution.py
+++ b/solution.py
@@ -7,6 +7,28 @@
 rope_base = 160000.0
 norm_eps = 1e-05
 score_scale = 0.125
+
+
+def joined_along(blocks, dim):
+    blocks = jnp.moveaxis(blocks, 0, dim)
+    shape = blocks.shape
+    return blocks.reshape(*shape[:dim], shape[dim] * shape[dim + 1], *shape[dim + 2 :])
+
+
+def collected_by_bits(x, axis):
+    size = lax.axis_size(axis)
+    pieces = x[None]
+    for level in range(size.bit_length() - 1):
+        stride = 1 << level
+        other = lax.ppermute(pieces, axis, [(i, i ^ stride) for i in range(size)])
+        both = jnp.stack([pieces, other])
+        upper = lax.axis_index(axis) >> level & 1
+        pieces = jnp.where(upper == 0, both, both[::-1]).reshape(-1, *x.shape)
+    return pieces
+
+
+def doubled_up(x, axis, dim):
+    return joined_along(collected_by_bits(x, axis), dim)
 
 
 def positions(length_row, index_rows):
@@ -161,7 +183,7 @@
         lax.all_gather(shards[2], ("fsdp", "ctx"), axis=0, tiled=True),
         lax.all_gather(shards[3], ("fsdp", "ctx"), axis=0, tiled=True),
         lax.all_gather(shards[4], ("fsdp", "ctx"), axis=0, tiled=True),
-        lax.all_gather(shards[5], ("fsdp", "ctx"), axis=1, tiled=True),
+        doubled_up(shards[5], ("fsdp", "ctx"), 1),
     )
     index_rows = jnp.arange(group_rows, dtype=jnp.int32)
     segment, group_places = positions(lengths[0], index_rows)

time: 651 us -> 616 us (0.946)
  waiting for transfers between devices: 433 us -> 380 us
  starting transfers between devices: 28.6 us -> 36.5 us
  other arithmetic: 19.8 us -> 27.4 us
    all_gather x1 -> x0, waiting for transfers between devices: 53.2 us -> none  [local(): lax.all_gather(shards[5], ('fsdp', 'ctx'), axis=1, tiled=True)]
    ppermute x0 -> x5, waiting for transfers between devices: none -> 45.7 us  [collected_by_bits(): other = lax.ppermute(pieces, axis, [(i, i ^ stride) for i in range(size)])]
    all_gather x1, waiting for transfers between devices: 17.7 us -> 0.01 us  [local(): lax.all_gather(shards[1], ('fsdp', 'ctx'), axis=0, tiled=True)]
    all_gather x1, waiting for transfers between devices: 14.8 us -> 0.01 us  [local(): lax.all_gather(shards[2], ('fsdp', 'ctx'), axis=0, tiled=True)]
    all_gather x1, waiting for transfers between devices: 58.2 us -> 48.7 us  [local(): lax.all_gather(shards[4], ('fsdp', 'ctx'), axis=0, tiled=True)]
    ppermute x0 -> x5, starting transfers between devices: none -> 7.46 us  [collected_by_bits(): other = lax.ppermute(pieces, axis, [(i, i ^ stride) for i in range(size)])]
    unnamed x6 -> x5, waiting for transfers between devices: 271 us -> 269 us
  transfers between devices with their start and end apart: 13 -> 17, of which waited for: 11 -> 12; matrix products, arithmetic and copies ran while one was open for 7% -> 9% of each run, Pallas kernels for 0% -> 0%
where the time goes in v1:
time: 616 us; the launch traced here: 614 us
  waiting for transfers between devices  380 us (62%)
  blocking collectives  82.7 us (13%)
  matrix products  39.6 us (6%)
  starting transfers between devices  36.5 us (6%)
  local copies, waits for them, and re-layouts  33 us (5%)
  other arithmetic  27.4 us (4%)
  between operations  14.6 us (2%)
    unnamed x5, waiting for transfers between devices  269 us
    unnamed x2, blocking collectives  82.7 us
    all_gather x1, waiting for transfers between devices, local(): lax.all_gather(shards[4], ('fsdp', 'ctx'), axis=0, tiled=True)  48.7 us
    ppermute x5, waiting for transfers between devices, collected_by_bits(): other = lax.ppermute(pieces, axis, [(i, i ^ stride) for i in range(size)])  45.7 us
    dot_general x10, matrix products, contract_rows(): lax.dot_general(left_side, right_side, (((0,), (0,)), ((), ())), preferre...  17 us
  transfers between devices with their start and end apart: 17, of which 12 were waited for; matrix products, arithmetic and copies ran while one was open for 9% of the time, Pallas kernels for 0%

profile of v1, /device:TPU:0, one launch (start us, length us, event | category | flops | bytes accessed | tf_op | source)
XLA Modules:
  0.0 613.9 jit_solution(12159003029157022318)
XLA Ops:
  13.9 42.4 %all-reduce.6 = (bf16[768]{0:T(1024)(128)(2,1)S(1)}, bf16[768]{0:T(1024)(128)(2,1)S(1)}) all-reduce(bf16[768]{0:T(1024)(128)(2,1)S(1)} %dynamic-update-slice, bf16[768]{0:T(1024)(128)(2,1)S(1)} %dynamic-update-slice.1), channel_id=1, replica_groups=mesh['fsdp'=8,'ctx'=4] {'fsdp','ctx'}, use_global_device_ids=true, to_apply=%add | all-reduce | flops 1536 | bytes 6144
  57.3 2.3 collective-permute-start.1
  59.7 5.4 collective-permute-done.1
  65.2 1.9 collective-permute-start.2
  67.1 4.1 collective-permute-done.2
  73.0 9.6 %collective-permute-done.3 = bf16[8,1152,24]{1,2,0:T(8,128)(2,1)S(1)} collective-permute-done((bf16[8,1152,24]{1,2,0:T(8,128)(2,1)S(1)}, bf16[8,1152,24]{1,2,0:T(8,128)(2,1)S(1)}, u32[]{:S(2)}, u32[]{:S(2)}) %collective-permute-start.3) | collective-permute-done | bytes 442400 | tf_op jit(solution)/shard_map/ppermute | solution.py:23
  82.8 1.4 collective-permute-start.4
  84.3 2.7 fusion.87
  92.1 1.7 copy.110
  93.9 3.9 all-to-all-start
  97.8 26.7 %collective-permute-done.4 = bf16[16,1152,24]{1,2,0:T(8,128)(2,1)} collective-permute-done((bf16[16,1152,24]{1,2,0:T(8,128)(2,1)S(1)}, bf16[16,1152,24]{1,2,0:T(8,128)(2,1)}, u32[]{:S(2)}, u32[]{:S(2)}) %collective-permute-start.4) | collective-permute-done | bytes 884768 | tf_op jit(solution)/shard_map/ppermute | solution.py:23
  124.5 2.6 pad_maximum_fusion.1
  128.7 3.4 all-to-all-start.1
  132.1 5.8 all-to-all-done.1
  138.0 3.4 all-to-all-start.2
  143.1 3.5 all-to-all-done.2
  149.2 3.4 all-to-all-start.3
  152.6 3.6 reverse_select_fusion
  156.2 1.6 all-to-all-done.3
  158.6 1.8 fusion.97
  161.6 48.7 %all-gather.8.cloned.1.call-done = bf16[768,2304]{1,0:T(8,128)(2,1)} async-done(((bf16[24,2304]{1,0:T(8,128)(2,1)}), bf16[768,2304]{1,0:T(8,128)(2,1)}) %all-gather.8.cloned.1.call-update) | async-done | bytes 3538960 | tf_op jit(solution)/shard_map/all_gather | solution.py:185
  210.3 2.9 fusion.89
  214.2 1.6 copy-done.9
  215.9 1.9 multiply_reduce_fusion
  219.2 2.2 convolution_convert_fusion
  221.4 1.7 copy.121
  223.1 4.2 all-to-all-start.4
  227.3 5.1 fusion.37
  244.9 3.4 all-to-all-start.7
  249.5 1.6 fusion.34
  251.8 1.8 all-to-all-done.7
  253.6 3.4 all-to-all-start.5
  257.0 2.5 convolution_bitcast_fusion
  260.2 2.0 all-to-all-done.5
  262.2 4.0 all-to-all-start.6
  266.3 3.2 fusion.49
  269.5 2.1 all-to-all-done.6
  271.6 2.5 fusion.39
  275.8 7.4 %pad_maximum_fusion = f32[768,6528]{1,0:T(8,128)} fusion(f32[768,1152]{1,0:T(8,128)S(1)} %copy-done, f32[768,2304]{1,0:T(8,128)S(1)} %bitcast.140, f32[768,768]{1,0:T(8,128)S(1)} %copy-done.1, f32[768,2304]{1,0:T(8,128)S(1)} %fusion.39), kind=kLoop, calls=%fused_computation | loop fusion | flops 15040512 | bytes 40108032 | tf_op jit(solution)/shard_map/concatenate | solution.py:260
  283.3 1.4 copy-done.5
  284.7 2.6 fusion.6
  287.3 4.2 fusion.31
  291.6 40.3 %all-reduce.5 = (f32[768]{0:T(1024)S(1)}, f32[768]{0:T(1024)S(1)}) all-reduce(f32[768]{0:T(1024)S(1)} %get-tuple-element.10, f32[768]{0:T(1024)S(1)} %copy-done.43), channel_id=2, replica_groups=mesh['fsdp'=8,'ctx'=4] {'fsdp','ctx'}, use_global_device_ids=true, to_apply=%region_21.22.clone | all-reduce | flops 1536 | bytes 12288
  333.0 1.9 fusion.30
  334.9 267.4 %all-reduce.9.cloned.1.call-done = f32[768,6528]{1,0:T(8,128)} async-done(((f32[768,6528]{1,0:T(8,128)}), f32[768,6528]{1,0:T(8,128)}) %all-reduce.9.cloned.1.call-update) | async-done | bytes 20054032
  602.3 1.6 dynamic-slice.4
  603.9 1.6 dynamic-slice_bitcast_fusion
  605.5 1.9 fusion.90
  (212 shorter events, 43.1 us)
Async XLA Ops:
  7.2 50.0 %copy-start.33 = (bf16[1152,24]{0,1:T(8,128)(2,1)S(1)}, bf16[1152,24]{0,1:T(8,128)(2,1)}, u32[]{:S(2)}) copy-start(bf16[1152,24]{0,1:T(8,128)(2,1)} %param.16) | copy-start | bytes 165892
  7.2 52.4 %copy-start.2 = (bf16[128,768]{1,0:T(8,128)(2,1)S(1)}, bf16[128,768]{1,0:T(8,128)(2,1)}, u32[]{:S(2)}) copy-start(bf16[128,768]{1,0:T(8,128)(2,1)} %param.9) | copy-start | bytes 589828
  7.2 77.1 %all-gather.4.cloned.1.call-start = ((), (), s32[]{:S(2)}) async-start(), calls=%async_computation.8 | async-start | bytes 3649536 | tf_op jit(solution)/shard_map/all_gather | solution.py:182
  7.9 148.3 %all-gather.6.cloned.1.call-start = ((), (), s32[]{:S(2)}) async-start(), calls=%async_computation.9 | async-start | bytes 1216512 | tf_op jit(solution)/shard_map/all_gather | solution.py:183
  8.7 201.7 %all-gather.8.cloned.1.call-start = ((), (), s32[]{:S(2)}) async-start(), calls=%async_computation.10 | async-start | bytes 3649536 | tf_op jit(solution)/shard_map/all_gather | solution.py:185
  8.7 48.5 %collective-permute-start = (bf16[1,1152,24]{1,2,0:T(8,128)(2,1)}, bf16[1,1152,24]{1,2,0:T(8,128)(2,1)S(1)}, u32[]{:S(2)}, u32[]{:S(2)}) collective-permute-start(bf16[1,1152,24]{1,2,0:T(8,128)(2,1)} %bitcast.169), channel_id=1, source_target_pairs={{0,1},{1,0},{2,3},{3,2},{4,5},{5,4},{6,7},{7,6},{8,9},{9,8},{10,11... | collective-permute-start | bytes 165896 | tf_op jit(solution)/shard_map/ppermute | solution.py:23
  57.3 7.8 %collective-permute-start.1 = (bf16[2,1152,24]{1,2,0:T(8,128)(2,1)S(1)}, bf16[2,1152,24]{1,2,0:T(8,128)(2,1)S(1)}, u32[]{:S(2)}, u32[]{:S(2)}) collective-permute-start(bf16[2,1152,24]{1,2,0:T(8,128)(2,1)S(1)} %get-tuple-element.42), channel_id=1, source_target_pairs={{0,2},{1,3},{2,0},{3,1},{4,6},{5,7},{6,4},{7,5},{8,10},{9,11},{10,... | collective-permute-start | bytes 331784 | tf_op jit(solution)/shard_map/ppermute | solution.py:23
  65.2 6.0 collective-permute-start.2
  67.1 17.2 %copy-start.36 = (f32[128]{0:T(128)}, f32[128]{0:T(128)S(1)}, u32[]{:S(2)}) copy-start(f32[128]{0:T(128)S(1)} %broadcast_multiply_fusion.9) | copy-start | bytes 1540
  71.3 11.3 %collective-permute-start.3 = (bf16[8,1152,24]{1,2,0:T(8,128)(2,1)S(1)}, bf16[8,1152,24]{1,2,0:T(8,128)(2,1)S(1)}, u32[]{:S(2)}, u32[]{:S(2)}) collective-permute-start(bf16[8,1152,24]{1,2,0:T(8,128)(2,1)S(1)} %bitcast.145), channel_id=1, source_target_pairs={{0,8},{1,9},{2,10},{3,11},{4,12},{5,13},{6,14},{7,15},{8,0},{9,1},... | collective-permute-start | bytes 1327112 | tf_op jit(solution)/shard_map/ppermute | solution.py:23
  73.0 11.2 %copy-start.40 = (f32[128]{0:T(128)}, f32[128]{0:T(128)S(1)}, u32[]{:S(2)}) copy-start(f32[128]{0:T(128)S(1)} %add_rsqrt_fusion.1) | copy-start | bytes 1540
  82.8 41.6 %collective-permute-start.4 = (bf16[16,1152,24]{1,2,0:T(8,128)(2,1)S(1)}, bf16[16,1152,24]{1,2,0:T(8,128)(2,1)}, u32[]{:S(2)}, u32[]{:S(2)}) collective-permute-start(bf16[16,1152,24]{1,2,0:T(8,128)(2,1)S(1)} %bitcast.143), channel_id=1, source_target_pairs={{0,16},{1,17},{2,18},{3,19},{4,20},{5,21},{6,22},{7,23},{8,24},{9,... | collective-permute-start | bytes 2654216 | tf_op jit(solution)/shard_map/ppermute | solution.py:23
  93.9 34.9 %all-to-all-start = ((bf16[128,4,192]{0,2,1:T(8,128)(2,1)}), bf16[128,4,192]{0,2,1:T(8,128)(2,1)S(1)}, u32[]{:S(2)}, u32[]{:S(2)}) async-start(bf16[128,4,192]{0,2,1:T(8,128)(2,1)} %bitcast.7), calls=%async_computation | async-start | bytes 393216 | tf_op jit(solution)/shard_map/all_to_all | solution.py:209
  128.7 9.2 %all-to-all-start.1 = ((bf16[128,4,192]{0,2,1:T(8,128)(2,1)}), bf16[128,4,192]{0,2,1:T(8,128)(2,1)S(1)}, u32[]{:S(2)}, u32[]{:S(2)}) async-start(bf16[128,4,192]{0,2,1:T(8,128)(2,1)} %bitcast.11), calls=%async_computation.1 | async-start | bytes 393216 | tf_op jit(solution)/shard_map/all_to_all | solution.py:210
  132.1 10.4 %copy-start.16 = (bf16[512,192]{0,1:T(8,128)(2,1)}, bf16[512,192]{0,1:T(8,128)(2,1)S(1)}, u32[]{:S(2)}) copy-start(bf16[512,192]{0,1:T(8,128)(2,1)S(1)} %copy_bitcast_fusion.2) | copy-start | bytes 589828
  138.0 8.6 %all-to-all-start.2 = ((bf16[128,4,192]{0,2,1:T(8,128)(2,1)}), bf16[128,4,192]{0,2,1:T(8,128)(2,1)S(1)}, u32[]{:S(2)}, u32[]{:S(2)}) async-start(bf16[128,4,192]{0,2,1:T(8,128)(2,1)} %bitcast.13), calls=%async_computation.2 | async-start | bytes 393216 | tf_op jit(solution)/shard_map/all_to_all | solution.py:211
  143.1 4.4 copy-start.34
  149.2 8.6 %all-to-all-start.3 = ((bf16[4,128,192]{1,2,0:T(8,128)(2,1)}), bf16[4,128,192]{1,2,0:T(8,128)(2,1)S(1)}, u32[]{:S(2)}, u32[]{:S(2)}) async-start(bf16[4,128,192]{1,2,0:T(8,128)(2,1)} %copy_bitcast_fusion.4), calls=%async_computation.3 | async-start | bytes 393216 | tf_op jit(solution)/shard_map/all_to_all | solution.py:214
  210.3 2.9 copy-start.4
  210.3 2.9 copy-start.14
  213.2 2.6 copy-start.9
  213.2 2.6 copy-start.39
  214.2 3.5 copy-start.28
  214.2 3.5 copy-start.29
  223.1 9.4 %all-to-all-start.4 = ((bf16[128,4,192]{0,2,1:T(8,128)(2,1)}), bf16[128,4,192]{0,2,1:T(8,128)(2,1)}, u32[]{:S(2)}, u32[]{:S(2)}) async-start(bf16[128,4,192]{0,2,1:T(8,128)(2,1)} %bitcast.158), calls=%async_computation.4 | async-start | bytes 393216 | tf_op jit(solution)/shard_map/all_to_all | solution.py:236
  232.5 3.9 copy-start.35
  234.5 2.8 copy-start.12
  239.6 4.6 copy-start.32
  239.9 4.3 copy-start.31
  239.9 4.3 copy-start.30
  241.3 7.0 %copy-start.27 = (f32[512,64]{0,1:T(8,128)S(1)}, f32[512,64]{0,1:T(8,128)}, u32[]{:S(2)}) copy-start(f32[512,64]{0,1:T(8,128)} %get-tuple-element.44) | copy-start | bytes 393220
  244.9 8.6 %all-to-all-start.7 = ((bf16[4,128,192]{1,2,0:T(8,128)(2,1)}), bf16[4,128,192]{1,2,0:T(8,128)(2,1)S(1)}, u32[]{:S(2)}, u32[]{:S(2)}) async-start(bf16[4,128,192]{1,2,0:T(8,128)(2,1)} %pad_maximum_fusion.15), calls=%async_computation.7 | async-start | bytes 393216 | tf_op jit(solution)/shard_map/all_to_all | solution.py:255
  249.5 7.5 %copy-start.8 = (f32[128,2304]{1,0:T(8,128)S(1)}, f32[128,2304]{1,0:T(8,128)}, u32[]{:S(2)}) copy-start(f32[128,2304]{1,0:T(8,128)} %copy-done.7) | copy-start | bytes 3538948
  249.5 7.5 %copy-start.15 = (bf16[128,768]{1,0:T(8,128)(2,1)S(1)}, bf16[128,768]{1,0:T(8,128)(2,1)}, u32[]{:S(2)}) copy-start(bf16[128,768]{1,0:T(8,128)(2,1)} %param.17) | copy-start | bytes 589828
  253.6 5.9 copy-start.20
  253.6 8.6 %all-to-all-start.5 = ((bf16[4,128,192]{1,2,0:T(8,128)(2,1)}), bf16[4,128,192]{1,2,0:T(8,128)(2,1)S(1)}, u32[]{:S(2)}, u32[]{:S(2)}) async-start(bf16[4,128,192]{1,2,0:T(8,128)(2,1)} %copy.126), calls=%async_computation.5 | async-start | bytes 393216 | tf_op jit(solution)/shard_map/all_to_all | solution.py:253
  260.2 11.4 %copy-start.3 = (bf16[128,768]{1,0:T(8,128)(2,1)S(1)}, bf16[128,768]{1,0:T(8,128)(2,1)}, u32[]{:S(2)}) copy-start(bf16[128,768]{1,0:T(8,128)(2,1)} %param.9) | copy-start | bytes 589828
  260.2 11.4 %copy-start.37 = (f32[128]{0:T(128)S(1)}, f32[128]{0:T(128)}, u32[]{:S(2)}) copy-start(f32[128]{0:T(128)} %copy-done.36) | copy-start | bytes 1540
  260.2 11.4 %copy-start.41 = (f32[128]{0:T(128)S(1)}, f32[128]{0:T(128)}, u32[]{:S(2)}) copy-start(f32[128]{0:T(128)} %copy-done.40) | copy-start | bytes 1540
  262.2 4.0 copy-start.22
  262.2 9.4 %all-to-all-start.6 = ((bf16[4,128,192]{1,2,0:T(8,128)(2,1)}), bf16[4,128,192]{1,2,0:T(8,128)(2,1)}, u32[]{:S(2)}, u32[]{:S(2)}) async-start(bf16[4,128,192]{1,2,0:T(8,128)(2,1)} %copy.127), calls=%async_computation.6 | async-start | bytes 393216 | tf_op jit(solution)/shard_map/all_to_all | solution.py:254
  266.2 336.1 %all-reduce.9.cloned.1.call-start = ((), (), s32[]{:S(2)}) async-start(), calls=%async_computation.11 | async-start | bytes 40108032
  266.3 7.8 %slice-start = ((s8[7077888]{0:T(1024)(128)(4,1)}), s8[2883584]{0:T(1024)(128)(4,1)S(1)}, s32[]{:S(2)}) async-start(s8[7077888]{0:T(1024)(128)(4,1)} %bitcast.139), calls=%async_computation.12 | async-start | bytes 5767168
  271.6 3.6 copy-start
  271.6 4.2 copy-start.1
  283.3 4.1 copy-start.21
  283.3 4.0 copy-start.23
  287.3 4.2 copy-start.43
  (15 other events, 19.0 us)
Sparse Core Ops, SparseCore 0:
  10.9 64.5 all-gather.3
  78.4 70.0 all-gather.5
  151.4 58.8 all-gather.7
  283.4 318.8 all-reduce.8
